TPU v7x, 256 devices: a whole 4x4x8 slice. The times are simulated.
256 devices in a mesh: emb: 32 (over z_hi, y, core), wide: 8 (over x, z_lo).
Axes of the slice: x: 4, y: 4, z: 8 (z_hi: 4, z_lo: 2; z = z_hi * 2 + z_lo), core: 2. Of those that a mesh axis runs over, the one named last changes fastest.
Arguments:
- tables: bfloat16 [512, 512, 256], P('emb'), may hold values from -3 to 3
- bag_ids: int32 [8, 128, 512, 4], P('wide', None, 'emb'), may hold values from 0 to 511
- bag_lengths: int32 [8, 128, 512], P('wide', None, 'emb'), may hold values from 1 to 4
- slot_field: int32 [512], replicated, may hold values from 0 to 511, each once
- proj_y: bfloat16 [512, 256], replicated, may hold values from -0.25 to 0.25
- proj_p: bfloat16 [128, 512], replicated, may hold values from -0.25 to 0.25
- linear_w: bfloat16 [384, 512], replicated, may hold values from -0.25 to 0.25
- fm_gain: float32 [256], replicated, may hold values from 0.5 to 1.5
- w_up: bfloat16 [8192, 256], P('wide'), may hold values from -0.375 to 0.375
- w_down: bfloat16 [8192, 256], P('wide'), may hold values from -0.0625 to 0.0625
- out_gain: float32 [256], replicated, may hold values from 0.5 to 1.5
- cotangent: bfloat16 [8, 128, 512, 256], P('wide', 'emb'), may hold values from -6 to 6
Outputs:
- layer_out: bfloat16 [8, 128, 512, 256], P('wide', 'emb')
- pooled_grad: bfloat16 [8, 128, 512, 256], P('wide', None, 'emb')
- grad_up: float32 [8192, 256], P('wide')
- grad_down: float32 [8192, 256], P('wide')
Inputs may be any that keep to these rules, and one draw needn't show every extreme that they name: `bag_ids`: each id indexes a bucket of the table of its slot. `slot_field`: each field appears in exactly one slot.
All inputs are finite; a program needn't handle non-finite values.
Results may differ from a plain program's by a relative error of at most 0.008.
Values may be sent and summed in bfloat16 or wider, within the bound.
A program may use at most 128 MiB of HBM per device.

v0:
```python
import jax
import jax.numpy as jnp
from jax import lax
from jax.sharding import PartitionSpec as P

NF = 128
norm_eps = 1e-05


def layer_norm(values):
    centre = jnp.mean(values, axis=-1, keepdims=True)
    shifted = values - centre
    scale = lax.rsqrt(jnp.mean(shifted * shifted, axis=-1, keepdims=True) + norm_eps)
    return (shifted * scale, scale)


def norm_back(unit, scale, gain, upstream):
    scaled = upstream * gain
    return scale * (
        scaled
        - jnp.mean(scaled, axis=-1, keepdims=True)
        - unit * jnp.mean(scaled * unit, axis=-1, keepdims=True)
    )


def silu_back(values):
    sigma = jax.nn.sigmoid(values)
    return sigma * (1.0 + values * (1.0 - sigma))


def pool_bags(tables, ids, lengths):
    slots_here = tables.shape[0]
    bucket_count = tables.shape[1]
    flat_ids = ids + (jnp.arange(slots_here, dtype=jnp.int32) * bucket_count)[None, :, None]
    gathered = jnp.take(tables.reshape(slots_here * bucket_count, -1), flat_ids, axis=0)
    live = (jnp.arange(ids.shape[2], dtype=jnp.int32)[None, None, :] < lengths[:, :, None]).astype(
        jnp.bfloat16
    )
    return jnp.einsum("gfj,gfje->gfe", live, gathered, preferred_element_type=jnp.float32).astype(
        jnp.bfloat16
    )


def body(
    tables,
    bag_ids,
    bag_lengths,
    slot_field,
    proj_y,
    proj_p,
    linear_w,
    fm_gain,
    w_up,
    w_down,
    out_gain,
    cotangent,
):
    pooled = pool_bags(tables, bag_ids[0], bag_lengths[0])[None]
    received = lax.all_to_all(pooled, "emb", split_axis=1, concat_axis=2, tiled=True)
    slot_embeds = received[0]
    embeds = jnp.zeros_like(slot_embeds).at[:, slot_field].set(slot_embeds)
    samples = embeds.shape[0]
    crossed = jnp.einsum("bfe,fk->bek", embeds, proj_y, preferred_element_type=jnp.float32).astype(
        jnp.bfloat16
    )
    mixing = jnp.einsum("nf,bfe->bne", proj_p, embeds, preferred_element_type=jnp.float32).astype(
        jnp.bfloat16
    )
    inter = jnp.einsum("bne,bek->bnk", mixing, crossed, preferred_element_type=jnp.float32)
    inter_unit, inter_scale = layer_norm(inter)
    inter_norm = (inter_unit * fm_gain).astype(jnp.bfloat16)
    inter_rows = inter_norm.reshape(samples * NF, -1)
    row_total = inter_rows.shape[0]
    up_all, down_all = (
        lax.all_gather(w_up, "wide", axis=0, tiled=True),
        lax.all_gather(w_down, "wide", axis=0, tiled=True),
    )
    gate_pre = jnp.einsum("rk,hk->rh", inter_rows, up_all, preferred_element_type=jnp.float32)
    hidden = jax.nn.silu(gate_pre).astype(jnp.bfloat16)
    ff_rows = jnp.dot(hidden, down_all, preferred_element_type=jnp.float32)
    linear_out = jnp.einsum("lf,bfe->ble", linear_w, embeds, preferred_element_type=jnp.float32)
    summed = jnp.concatenate(
        [ff_rows.reshape(samples, NF, -1), linear_out], axis=1
    ) + embeds.astype(jnp.float32)
    summed_unit, summed_scale = layer_norm(summed)
    layer_out = (summed_unit * out_gain).astype(jnp.bfloat16)
    grad_summed = norm_back(summed_unit, summed_scale, out_gain, cotangent[0].astype(jnp.float32))
    grad_ff = grad_summed[:, :NF].astype(jnp.bfloat16)
    grad_lin = grad_summed[:, NF:].astype(jnp.bfloat16)
    grad_ff_rows = grad_ff.reshape(row_total, -1)
    grad_hidden = jnp.einsum(
        "re,he->rh", grad_ff_rows, down_all, preferred_element_type=jnp.float32
    )
    grad_gate = (grad_hidden * silu_back(gate_pre)).astype(jnp.bfloat16)
    grad_rows = jnp.dot(grad_gate, up_all, preferred_element_type=jnp.float32)
    rank_width = w_up.shape[1]
    up_term = jnp.einsum("rh,rk->hk", grad_gate, inter_rows, preferred_element_type=jnp.float32)
    down_term_part = jnp.einsum(
        "rh,re->he", hidden, grad_ff_rows, preferred_element_type=jnp.float32
    )
    both_terms = lax.psum_scatter(
        jnp.concatenate([up_term, down_term_part], axis=1), "wide", scatter_dimension=0, tiled=True
    )
    up_local = both_terms[:, :rank_width]
    down_local = both_terms[:, rank_width:]
    grad_up, grad_down = lax.psum((up_local, down_local), "emb")
    grad_norm = grad_rows.reshape(samples, NF, -1)
    grad_inter = norm_back(inter_unit, inter_scale, fm_gain, grad_norm).astype(jnp.bfloat16)
    grad_mixing = jnp.einsum(
        "bnk,bek->bne", grad_inter, crossed, preferred_element_type=jnp.float32
    ).astype(jnp.bfloat16)
    grad_crossed = jnp.einsum(
        "bne,bnk->bek", mixing, grad_inter, preferred_element_type=jnp.float32
    ).astype(jnp.bfloat16)
    grad_embeds = grad_summed + jnp.einsum(
        "lf,ble->bfe", linear_w, grad_lin, preferred_element_type=jnp.float32
    )
    grad_embeds = grad_embeds + jnp.einsum(
        "nf,bne->bfe", proj_p, grad_mixing, preferred_element_type=jnp.float32
    )
    grad_embeds = grad_embeds + jnp.einsum(
        "fk,bek->bfe", proj_y, grad_crossed, preferred_element_type=jnp.float32
    )
    grad_embeds = grad_embeds.astype(jnp.bfloat16)
    slot_grads = grad_embeds[:, slot_field]
    returned = lax.all_to_all(slot_grads[None], "emb", split_axis=2, concat_axis=1, tiled=True)
    return (layer_out[None], returned, grad_up, grad_down)


def solution(mesh):
    placed = (
        P("emb", None, None),
        P("wide", None, "emb", None),
        P("wide", None, "emb"),
        P(),
        P(),
        P(),
        P(),
        P(),
        P("wide", None),
        P("wide", None),
        P(),
        P("wide", "emb", None, None),
    )
    return jax.shard_map(
        body,
        mesh=mesh,
        in_specs=placed,
        out_specs=(
            P("wide", "emb", None, None),
            P("wide", None, "emb", None),
            P("wide", None),
            P("wide", None),
        ),
        check_vma=False,
    )
```

profile of v0, /device:TPU:1, one launch (start us, length us, event | category | flops | bytes accessed | tf_op | source)
XLA Modules:
  0.0 923.4 jit_solution(3896068090639616225)
XLA Ops:
  11.6 33.8 %gather_fusion = bf16[8192,256]{1,0:T(8,128)(2,1)} fusion(bf16[8192,256]{1,0:T(8,128)(2,1)} %bitcast.109, s32[8192]{0:T(1024)S(1)} %broadcast_clamp_fusion), kind=kCustom, calls=%fused_computation | custom fusion | bytes 8421376 | tf_op jit(solution)/shard_map/jit(_take)/gather | solution.py:35
  45.4 7.0 reshape.111
  53.4 8.1 fusion
  62.7 12.8 %all-to-all-start = ((bf16[1,128,16,256]{3,2,0,1:T(8,128)(2,1)}), bf16[1,128,16,256]{3,2,0,1:T(8,128)(2,1)S(1)}, u32[]{:S(2)}, u32[]{:S(2)}) async-start(bf16[1,128,16,256]{3,2,0,1:T(8,128)(2,1)} %bitcast.108), calls=%async_computation | async-start | bytes 2097152 | tf_op jit(solution)/shard_map/all_to_all | solution.py:59
  75.6 1.3 copy.76
  76.9 38.6 %all-to-all-done = bf16[1,128,16,256]{3,2,0,1:T(8,128)(2,1)S(1)} async-done(((bf16[1,128,16,256]{3,2,0,1:T(8,128)(2,1)}), bf16[1,128,16,256]{3,2,0,1:T(8,128)(2,1)S(1)}, u32[]{:S(2)}, u32[]{:S(2)}) %all-to-all-start) | async-done | bytes 1048608 | tf_op jit(solution)/shard_map/all_to_all | solution.py:59
  116.7 13.6 %scatter_fusion = bf16[4,512,256]{2,0,1:T(4,128)(2,1)S(1)} fusion(bf16[4,512,256]{2,0,1:T(4,128)(2,1)S(1)} %broadcast_in_dim.20, s32[512]{0:T(512)S(1)} %compare_select_fusion.2, bf16[512,4,256]{2,1,0:T(4,128)(2,1)S(1)} %copy.69), kind=kCustom, calls=%fused_computation.2 | custom fusion | bytes 3147776 | tf_op jit(solution)/shard_map/scatter | solution.py:61
  131.2 1.3 convolution_convert_fusion.3
  132.6 1.5 convolution_convert_fusion
  136.0 1.9 convolution_bitcast_fusion
  137.9 13.1 %multiply_convert_fusion.1 = (bf16[512,8192]{1,0:T(8,128)(2,1)}, f32[512,8192]{1,0:T(8,128)}) fusion(bf16[512,256]{1,0:T(8,128)(2,1)S(1)} %bitcast.114, bf16[8192,256]{1,0:T(8,128)(2,1)} %all-gather.3.cloned.1.call-done), kind=kOutput, calls=%fused_computation.5 | convolution fusion | flops 2168455168 | bytes 29622272 | tf_op jit(solution)/shard_map/rk,hk->rh/dot_general | solution.py:78
  151.0 73.2 %all-gather.5.cloned.1.call-done = bf16[8192,256]{1,0:T(8,128)(2,1)} async-done(((bf16[1024,256]{1,0:T(8,128)(2,1)}), bf16[8192,256]{1,0:T(8,128)(2,1)}) %all-gather.5.cloned.1.call-update) | async-done | bytes 4194320 | tf_op jit(solution)/shard_map/all_gather | solution.py:76
  224.3 6.9 fusion.29
  232.2 1.9 fusion.26
  235.1 1.9 fusion.22
  238.1 5.8 fusion.31
  244.0 13.6 %multiply_convert_fusion = bf16[512,8192]{1,0:T(8,128)(2,1)} fusion(f32[512,8192]{1,0:T(8,128)} %get-tuple-element.33, bf16[512,256]{1,0:T(8,128)(2,1)S(1)} %bitcast.117, bf16[8192,256]{1,0:T(8,128)(2,1)} %all-gather.5.cloned.1.call-done), kind=kOutput, calls=%fused_computation.4 | convolution fusion | flops 2185232384 | bytes 29622272 | tf_op jit(solution)/shard_map/re,he->rh/dot_general | solution.py:91
  257.6 6.0 fusion.30
  263.6 6.2 pad_maximum_fusion
  271.0 7.1 multiply_reduce_fusion.2
  279.5 2.0 fusion.12
  281.5 3.4 fusion.16
  284.9 314.3 %reduce-scatter.2.cloned.1.call-done = f32[1024,512]{0,1:T(8,128)} async-done(((f32[8192,512]{0,1:T(8,128)}), f32[1024,512]{0,1:T(8,128)}) %reduce-scatter.2.cloned.1.call-update) | async-done | bytes 2097168 | tf_op jit(solution)/shard_map/reduce_scatter | solution.py:101
  599.2 3.1 fusion.27
  602.4 4.5 fusion.10
  606.9 1.8 copy.79
  608.6 3.1 gather_fusion.1
  611.7 9.3 %all-to-all-start.1 = ((bf16[1,4,512,256]{3,1,0,2:T(4,128)(2,1)}), bf16[1,4,512,256]{3,1,0,2:T(4,128)(2,1)S(1)}, u32[]{:S(2)}, u32[]{:S(2)}) async-start(bf16[1,4,512,256]{3,1,0,2:T(4,128)(2,1)} %bitcast.27), calls=%async_computation.1 | async-start | bytes 2097152 | tf_op jit(solution)/shard_map/all_to_all | solution.py:126
  622.4 22.7 %all-to-all-done.1 = bf16[1,4,512,256]{3,1,0,2:T(4,128)(2,1)S(1)} async-done(((bf16[1,4,512,256]{3,1,0,2:T(4,128)(2,1)}), bf16[1,4,512,256]{3,1,0,2:T(4,128)(2,1)S(1)}, u32[]{:S(2)}, u32[]{:S(2)}) %all-to-all-start.1) | async-done | bytes 1048608 | tf_op jit(solution)/shard_map/all_to_all | solution.py:126
  646.3 265.5 %all-reduce.3.cloned.1.call-done = (f32[1024,256]{0,1:T(8,128)}, f32[1024,256]{0,1:T(8,128)}) async-done(((f32[1024,256]{0,1:T(8,128)}, f32[1024,256]{0,1:T(8,128)}), (f32[1024,256]{0,1:T(8,128)}, f32[1024,256]{0,1:T(8,128)})) %all-reduce.3.cloned.1.call-update) | async-done | bytes 2097168 | tf_op jit(solution)/shard_map/psum | solution.py:106
  911.8 2.5 copy.84
  914.3 2.5 copy.85
  (101 shorter events, 19.0 us)
Async XLA Ops:
  7.2 128.8 %copy-start = (bf16[384,512]{1,0:T(8,128)(2,1)S(1)}, bf16[384,512]{1,0:T(8,128)(2,1)}, u32[]{:S(2)}) copy-start(bf16[384,512]{1,0:T(8,128)(2,1)} %param.18) | copy-start | bytes 1179652
  7.2 130.7 %all-gather.3.cloned.1.call-start = ((), (), s32[]{:S(2)}) async-start(), calls=%async_computation.3 | async-start | bytes 4718592 | tf_op jit(solution)/shard_map/all_gather | solution.py:75
  7.9 216.3 %all-gather.5.cloned.1.call-start = ((), (), s32[]{:S(2)}) async-start(), calls=%async_computation.4 | async-start | bytes 4718592 | tf_op jit(solution)/shard_map/all_gather | solution.py:76
  45.4 7.6 copy-start.26
  61.5 14.1 %copy-start.13 = (bf16[1,4,512,256]{3,2,1,0:T(8,128)(2,1)S(1)}, bf16[1,4,512,256]{3,2,1,0:T(8,128)(2,1)}, u32[]{:S(2)}) copy-start(bf16[1,4,512,256]{3,2,1,0:T(8,128)(2,1)} %param.23) | copy-start | bytes 3145732
  61.5 15.4 %copy-start.27 = (s32[512]{0:T(512)S(1)}, s32[512]{0:T(512)}, u32[]{:S(2)}) copy-start(s32[512]{0:T(512)} %param.15) | copy-start | bytes 6148
  62.7 52.7 %all-to-all-start = ((bf16[1,128,16,256]{3,2,0,1:T(8,128)(2,1)}), bf16[1,128,16,256]{3,2,0,1:T(8,128)(2,1)S(1)}, u32[]{:S(2)}, u32[]{:S(2)}) async-start(bf16[1,128,16,256]{3,2,0,1:T(8,128)(2,1)} %bitcast.108), calls=%async_computation | async-start | bytes 2097152 | tf_op jit(solution)/shard_map/all_to_all | solution.py:59
  75.5 523.7 %reduce-scatter.2.cloned.1.call-start = ((), (), s32[]{:S(2)}) async-start(), calls=%async_computation.5 | async-start | bytes 18874368 | tf_op jit(solution)/shard_map/reduce_scatter | solution.py:101
  76.9 39.8 %copy-start.21 = (s32[512]{0:T(512)}, s32[512]{0:T(512)S(1)}, u32[]{:S(2)}) copy-start(s32[512]{0:T(512)S(1)} %compare_select_fusion.2) | copy-start | bytes 6148
  130.2 5.5 copy-start.23
  132.6 3.4 copy-start.9
  134.0 1.9 copy-start.5
  134.4 0.8 copy-start.3
  134.4 0.8 copy-start.17
  136.0 15.0 %copy-start.11 = (bf16[4,128,256]{2,1,0:T(8,128)(2,1)}, bf16[4,128,256]{2,1,0:T(8,128)(2,1)S(1)}, u32[]{:S(2)}) copy-start(bf16[4,128,256]{2,1,0:T(8,128)(2,1)S(1)} %multiply_convert_fusion.4) | copy-start | bytes 786436
  232.2 2.3 copy-start.1
  232.2 2.3 copy-start.25
  235.1 1.9 copy-start.15
  235.1 1.9 copy-start.16
  237.0 1.0 copy-start.8
  244.0 13.6 %copy-start.12 = (bf16[4,128,256]{2,1,0:T(8,128)(2,1)S(1)}, bf16[4,128,256]{2,1,0:T(8,128)(2,1)}, u32[]{:S(2)}) copy-start(bf16[4,128,256]{2,1,0:T(8,128)(2,1)} %copy-done.11) | copy-start | bytes 786436
  269.7 1.3 copy-start.24
  269.7 642.0 %all-reduce.3.cloned.1.call-start = ((), (), s32[]{:S(2)}) async-start(), calls=%async_computation.6 | async-start | bytes 4194304 | tf_op jit(solution)/shard_map/psum | solution.py:106
  271.0 7.1 copy-start.4
  271.0 7.1 copy-start.18
  271.0 7.1 copy-start.20
  271.0 8.5 copy-start.6
  271.0 8.5 copy-start.14
  278.8 0.7 copy-start.10
  281.5 320.9 %copy-start.2 = (bf16[1,4,512,256]{2,3,1,0:T(8,128)(2,1)S(1)}, bf16[1,4,512,256]{2,3,1,0:T(8,128)(2,1)}, u32[]{:S(2)}) copy-start(bf16[1,4,512,256]{2,3,1,0:T(8,128)(2,1)} %copy.76) | copy-start | bytes 3145732
  606.9 14.2 %copy-start.7 = (bf16[1,4,512,256]{2,3,1,0:T(8,128)(2,1)S(1)}, bf16[1,4,512,256]{2,3,1,0:T(8,128)(2,1)}, u32[]{:S(2)}) copy-start(bf16[1,4,512,256]{2,3,1,0:T(8,128)(2,1)} %get-tuple-element.27) | copy-start | bytes 3145732
  611.7 33.3 %all-to-all-start.1 = ((bf16[1,4,512,256]{3,1,0,2:T(4,128)(2,1)}), bf16[1,4,512,256]{3,1,0,2:T(4,128)(2,1)S(1)}, u32[]{:S(2)}, u32[]{:S(2)}) async-start(bf16[1,4,512,256]{3,1,0,2:T(4,128)(2,1)} %bitcast.27), calls=%async_computation.1 | async-start | bytes 2097152 | tf_op jit(solution)/shard_map/all_to_all | solution.py:126
  (2 other events, 1.2 us)
Sparse Core Ops, SparseCore 0:
  9.8 119.3 all-gather.2
  131.0 93.2 all-gather.4
  269.9 329.3 reduce-scatter.1
  602.5 309.2 all-reduce.2
where the time goes:
time: 924 us; the launch traced here: 923 us
  waiting for transfers between devices  716 us (77%)
  local copies, waits for them, and re-layouts  81 us (9%)
  matrix products  75.5 us (8%)
  starting transfers between devices  22.2 us (2%)
  other arithmetic  14.7 us (2%)
  between operations  14.2 us (2%)
    reduce_scatter x1, waiting for transfers between devices, body(): lax.psum_scatter(jnp.concatenate([up_term, down_term_part], axis=1), 'wid...  314 us
    psum x1, waiting for transfers between devices, body(): grad_up, grad_down = lax.psum((up_local, down_local), 'emb')  265 us
    all_gather x1, waiting for transfers between devices, body(): lax.all_gather(w_down, 'wide', axis=0, tiled=True)  73.2 us
    gather x2, local copies, waits for them, and re-layouts, pool_bags(): jnp.take(tables.reshape(slots_here * bucket_count, -1), flat_ids, axis=0)  40.8 us
    all_to_all x1, waiting for transfers between devices, body(): lax.all_to_all(pooled, 'emb', split_axis=1, concat_axis=2, tiled=True)  38.6 us
    all_to_all x1, waiting for transfers between devices, body(): lax.all_to_all(slot_grads[None], 'emb', split_axis=2, concat_axis=1, tile...  22.7 us
  transfers between devices with their start and end apart: 6, of which 5 were waited for; matrix products, arithmetic and copies ran while one was open for 12% of the time, Pallas kernels for 0%

commit v1 on v0

--- a/solution.py
+++ b/solution.py
@@ -73,7 +73,15 @@
     row_total = inter_rows.shape[0]
     up_all, down_all = (
         lax.all_gather(w_up, "wide", axis=0, tiled=True),
-        lax.all_gather(w_down, "wide", axis=0, tiled=True),
+        jnp.concatenate(
+            lax.all_to_all(
+                jnp.stack(lax.axis_size("wide") * [w_down]),
+                concat_axis=0,
+                split_axis=0,
+                axis_name="wide",
+            ),
+            0,
+        ),
     )
     gate_pre = jnp.einsum("rk,hk->rh", inter_rows, up_all, preferred_element_type=jnp.float32)
     hidden = jax.nn.silu(gate_pre).astype(jnp.bfloat16)

time: 924 us -> 872 us (0.944)
  waiting for transfers between devices: 716 us -> 619 us
  blocking collectives: 0 us -> 52.5 us
    all_gather x1 -> x0, waiting for transfers between devices: 73.2 us -> none  [body(): lax.all_gather(w_down, 'wide', axis=0, tiled=True)]
    all_to_all x0 -> x1, blocking collectives: none -> 52.5 us  [body(): lax.all_to_all(pooled, 'emb', split_axis=1, concat_axis=2, tiled=True)]
    all_to_all x1, waiting for transfers between devices: 38.6 us -> 17.3 us  [body(): lax.all_to_all(jnp.stack(lax.axis_size('wide') * [w_down]), concat_axis=0...]
  transfers between devices with their start and end apart: 6 -> 5, of which waited for: 5 -> 4; matrix products, arithmetic and copies ran while one was open for 12% -> 13% of each run, Pallas kernels for 0% -> 0%
where the time goes in v1:
time: 872 us; the launch traced here: 871 us
  waiting for transfers between devices  619 us (71%)
  local copies, waits for them, and re-layouts  81.6 us (9%)
  matrix products  75.7 us (9%)
  blocking collectives  52.5 us (6%)
  starting transfers between devices  14.7 us (2%)
  between operations  14.2 us (2%)
  other arithmetic  13 us (1%)
    reduce_scatter x1, waiting for transfers between devices, body(): lax.psum_scatter(jnp.concatenate([up_term, down_term_part], axis=1), 'wid...  313 us
    psum x1, waiting for transfers between devices, body(): grad_up, grad_down = lax.psum((up_local, down_local), 'emb')  265 us
    all_to_all x1, blocking collectives, body(): lax.all_to_all(pooled, 'emb', split_axis=1, concat_axis=2, tiled=True)  52.5 us
    gather x2, local copies, waits for them, and re-layouts, pool_bags(): jnp.take(tables.reshape(slots_here * bucket_count, -1), flat_ids, axis=0)  40.7 us
    all_to_all x1, waiting for transfers between devices, body(): lax.all_to_all(slot_grads[None], 'emb', split_axis=2, concat_axis=1, tile...  22.7 us
  transfers between devices with their start and end apart: 5, of which 4 were waited for; matrix products, arithmetic and copies ran while one was open for 13% of the time, Pallas kernels for 0%

profile of v1, /device:TPU:1, one launch (start us, length us, event | category | flops | bytes accessed | tf_op | source)
XLA Modules:
  0.0 871.0 jit_solution(16606223794085552465)
XLA Ops:
  10.8 33.7 %gather_fusion = bf16[8192,256]{1,0:T(8,128)(2,1)} fusion(bf16[8192,256]{1,0:T(8,128)(2,1)} %bitcast.112, s32[8192]{0:T(1024)S(1)} %broadcast_clamp_fusion), kind=kCustom, calls=%fused_computation | custom fusion | bytes 8421376 | tf_op jit(solution)/shard_map/jit(_take)/gather | solution.py:35
  44.5 7.0 reshape.115
  52.5 8.1 fusion
  60.9 52.5 %all_to_all.38 = bf16[1,128,16,256]{3,2,0,1:T(8,128)(2,1)S(1)} all-to-all(bf16[1,128,16,256]{3,2,0,1:T(8,128)(2,1)S(1)} %bitcast.114), channel_id=1, replica_groups=mesh['emb'=32,'wide'=8] {'emb'}, dimensions={1} | all-to-all | bytes 2097152 | tf_op jit(solution)/shard_map/all_to_all | solution.py:59
  113.4 2.3 stack.2
  115.8 4.7 all-to-all-start.1
  120.8 1.3 copy.76
  123.3 13.6 %scatter_fusion = bf16[4,512,256]{2,0,1:T(4,128)(2,1)S(1)} fusion(bf16[4,512,256]{2,0,1:T(4,128)(2,1)S(1)} %broadcast_in_dim.20, s32[512]{0:T(512)S(1)} %compare_select_fusion.2, bf16[512,4,256]{2,1,0:T(4,128)(2,1)S(1)} %copy.69), kind=kCustom, calls=%fused_computation.2 | custom fusion | bytes 3147776 | tf_op jit(solution)/shard_map/scatter | solution.py:61
  137.9 1.3 convolution_convert_fusion.3
  139.2 1.5 convolution_convert_fusion
  142.7 1.9 convolution_bitcast_fusion
  144.6 13.1 %multiply_convert_fusion.1 = (bf16[512,8192]{1,0:T(8,128)(2,1)}, f32[512,8192]{1,0:T(8,128)}) fusion(bf16[512,256]{1,0:T(8,128)(2,1)S(1)} %bitcast.119, bf16[8192,256]{1,0:T(8,128)(2,1)} %all-gather.2.cloned.1.call-done), kind=kOutput, calls=%fused_computation.5 | convolution fusion | flops 2168455168 | bytes 29622272 | tf_op jit(solution)/shard_map/rk,hk->rh/dot_general | solution.py:86
  157.7 17.3 %all-to-all-done.1 = bf16[8,1024,256]{2,1,0:T(8,128)(2,1)} async-done(((bf16[8,1024,256]{2,1,0:T(8,128)(2,1)}), bf16[8,1024,256]{2,1,0:T(8,128)(2,1)}, u32[]{:S(2)}, u32[]{:S(2)}) %all-to-all-start.1) | async-done | bytes 4194336 | tf_op jit(solution)/shard_map/all_to_all | solution.py:77
  175.0 7.3 fusion.29
  184.2 1.9 fusion.22
  187.2 5.8 fusion.31
  193.1 13.6 %multiply_convert_fusion = bf16[512,8192]{1,0:T(8,128)(2,1)} fusion(f32[512,8192]{1,0:T(8,128)} %get-tuple-element.33, bf16[512,256]{1,0:T(8,128)(2,1)S(1)} %bitcast.122, bf16[8192,256]{1,0:T(8,128)(2,1)} %bitcast.15), kind=kOutput, calls=%fused_computation.4 | convolution fusion | flops 2185232384 | bytes 29622272 | tf_op jit(solution)/shard_map/re,he->rh/dot_general | solution.py:99
  206.6 6.0 fusion.30
  212.6 6.1 pad_maximum_fusion
  220.0 7.1 multiply_reduce_fusion.2
  228.5 2.0 fusion.12
  230.6 3.2 fusion.16
  233.8 313.2 %reduce-scatter.2.cloned.1.call-done = f32[1024,512]{0,1:T(8,128)} async-done(((f32[8192,512]{0,1:T(8,128)}), f32[1024,512]{0,1:T(8,128)}) %reduce-scatter.2.cloned.1.call-update) | async-done | bytes 2097168 | tf_op jit(solution)/shard_map/reduce_scatter | solution.py:109
  547.0 3.1 fusion.27
  550.2 4.5 fusion.10
  554.7 1.8 copy.79
  556.5 3.1 gather_fusion.1
  559.5 9.3 %all-to-all-start.2 = ((bf16[1,4,512,256]{3,1,0,2:T(4,128)(2,1)}), bf16[1,4,512,256]{3,1,0,2:T(4,128)(2,1)S(1)}, u32[]{:S(2)}, u32[]{:S(2)}) async-start(bf16[1,4,512,256]{3,1,0,2:T(4,128)(2,1)} %bitcast.29), calls=%async_computation.2 | async-start | bytes 2097152 | tf_op jit(solution)/shard_map/all_to_all | solution.py:134
  570.2 22.7 %all-to-all-done.2 = bf16[1,4,512,256]{3,1,0,2:T(4,128)(2,1)S(1)} async-done(((bf16[1,4,512,256]{3,1,0,2:T(4,128)(2,1)}), bf16[1,4,512,256]{3,1,0,2:T(4,128)(2,1)S(1)}, u32[]{:S(2)}, u32[]{:S(2)}) %all-to-all-start.2) | async-done | bytes 1048608 | tf_op jit(solution)/shard_map/all_to_all | solution.py:134
  594.1 265.3 %all-reduce.3.cloned.1.call-done = (f32[1024,256]{0,1:T(8,128)}, f32[1024,256]{0,1:T(8,128)}) async-done(((f32[1024,256]{0,1:T(8,128)}, f32[1024,256]{0,1:T(8,128)}), (f32[1024,256]{0,1:T(8,128)}, f32[1024,256]{0,1:T(8,128)})) %all-reduce.3.cloned.1.call-update) | async-done | bytes 2097168 | tf_op jit(solution)/shard_map/psum | solution.py:114
  859.4 2.5 copy.84
  861.9 2.5 copy.85
  (103 shorter events, 17.4 us)
Async XLA Ops:
  7.2 135.5 %copy-start = (bf16[384,512]{1,0:T(8,128)(2,1)S(1)}, bf16[384,512]{1,0:T(8,128)(2,1)}, u32[]{:S(2)}) copy-start(bf16[384,512]{1,0:T(8,128)(2,1)} %param.18) | copy-start | bytes 1179652
  7.2 137.4 %all-gather.2.cloned.1.call-start = ((), (), s32[]{:S(2)}) async-start(), calls=%async_computation.4 | async-start | bytes 4718592 | tf_op jit(solution)/shard_map/all_gather | solution.py:75
  44.5 7.6 copy-start.28
  60.6 52.8 %copy-start.15 = (bf16[1024,256]{1,0:T(8,128)(2,1)S(1)}, bf16[1024,256]{1,0:T(8,128)(2,1)}, u32[]{:S(2)}) copy-start(bf16[1024,256]{1,0:T(8,128)(2,1)} %param.21) | copy-start | bytes 1572868
  115.8 5.0 copy-start.14
  115.8 6.3 copy-start.29
  115.8 59.2 %all-to-all-start.1 = ((bf16[8,1024,256]{2,1,0:T(8,128)(2,1)}), bf16[8,1024,256]{2,1,0:T(8,128)(2,1)}, u32[]{:S(2)}, u32[]{:S(2)}) async-start(bf16[8,1024,256]{2,1,0:T(8,128)(2,1)} %stack.2), calls=%async_computation.1 | async-start | bytes 8388608 | tf_op jit(solution)/shard_map/all_to_all | solution.py:77
  120.5 426.5 %reduce-scatter.2.cloned.1.call-start = ((), (), s32[]{:S(2)}) async-start(), calls=%async_computation.5 | async-start | bytes 18874368 | tf_op jit(solution)/shard_map/reduce_scatter | solution.py:109
  122.1 1.2 copy-start.23
  136.9 5.6 copy-start.25
  139.2 3.5 copy-start.10
  140.7 2.0 copy-start.6
  141.1 0.8 copy-start.3
  141.1 0.8 copy-start.19
  142.7 15.0 %copy-start.12 = (bf16[4,128,256]{2,1,0:T(8,128)(2,1)}, bf16[4,128,256]{2,1,0:T(8,128)(2,1)S(1)}, u32[]{:S(2)}) copy-start(bf16[4,128,256]{2,1,0:T(8,128)(2,1)S(1)} %multiply_convert_fusion.4) | copy-start | bytes 786436
  175.0 7.3 copy-start.5
  182.3 1.2 copy-start.1
  182.3 1.2 copy-start.27
  184.2 1.9 copy-start.17
  184.2 1.9 copy-start.18
  186.1 1.0 copy-start.9
  193.1 13.6 %copy-start.13 = (bf16[4,128,256]{2,1,0:T(8,128)(2,1)S(1)}, bf16[4,128,256]{2,1,0:T(8,128)(2,1)}, u32[]{:S(2)}) copy-start(bf16[4,128,256]{2,1,0:T(8,128)(2,1)} %copy-done.12) | copy-start | bytes 786436
  218.8 1.3 copy-start.26
  218.8 640.6 %all-reduce.3.cloned.1.call-start = ((), (), s32[]{:S(2)}) async-start(), calls=%async_computation.6 | async-start | bytes 4194304 | tf_op jit(solution)/shard_map/psum | solution.py:114
  220.0 7.1 copy-start.4
  220.0 7.1 copy-start.20
  220.0 7.1 copy-start.22
  220.0 8.5 copy-start.7
  220.0 8.5 copy-start.16
  230.5 319.6 %copy-start.2 = (bf16[1,4,512,256]{2,3,1,0:T(8,128)(2,1)S(1)}, bf16[1,4,512,256]{2,3,1,0:T(8,128)(2,1)}, u32[]{:S(2)}) copy-start(bf16[1,4,512,256]{2,3,1,0:T(8,128)(2,1)} %copy.76) | copy-start | bytes 3145732
  554.7 14.2 %copy-start.8 = (bf16[1,4,512,256]{2,3,1,0:T(8,128)(2,1)S(1)}, bf16[1,4,512,256]{2,3,1,0:T(8,128)(2,1)}, u32[]{:S(2)}) copy-start(bf16[1,4,512,256]{2,3,1,0:T(8,128)(2,1)} %get-tuple-element.27) | copy-start | bytes 3145732
  559.5 33.4 %all-to-all-start.2 = ((bf16[1,4,512,256]{3,1,0,2:T(4,128)(2,1)}), bf16[1,4,512,256]{3,1,0,2:T(4,128)(2,1)S(1)}, u32[]{:S(2)}, u32[]{:S(2)}) async-start(bf16[1,4,512,256]{3,1,0,2:T(4,128)(2,1)} %bitcast.29), calls=%async_computation.2 | async-start | bytes 2097152 | tf_op jit(solution)/shard_map/all_to_all | solution.py:134
  (3 other events, 1.9 us)
Sparse Core Ops, SparseCore 0:
  9.8 122.8 all-gather.1
  218.9 328.0 reduce-scatter.1
  550.3 309.0 all-reduce.2
